TPU v7x, 256 devices: a whole 4x4x8 slice. The times are simulated.
256 devices in a mesh: seq: 128 (over y, x_lo, z, core), tp: 2 (over x_hi).
Axes of the slice: x: 4 (x_hi: 2, x_lo: 2; x = x_hi * 2 + x_lo), y: 4, z: 8, core: 2. Of those that a mesh axis runs over, the one named last changes fastest.
Arguments:
- series: bfloat16 [32768, 2048], P(('seq', 'tp')), may hold values from -4 to 4
- norm_gain: float32 [2048], replicated, may hold values from 0.1 to 1.9
- w_query: bfloat16 [2048, 1024], P(None, 'tp'), may hold values from -0.5 to 0.5
- w_key: bfloat16 [2048, 1024], P(None, 'tp'), may hold values from -0.5 to 0.5
- w_value: bfloat16 [2048, 1024], P(None, 'tp'), may hold values from -0.125 to 0.125
- w_out: bfloat16 [1024, 2048], P('tp'), may hold values from -0.1875 to 0.1875
- out_grad: bfloat16 [32768, 2048], P(('seq', 'tp')), may hold values from -6 to 6
Outputs:
- layer_out: bfloat16 [32768, 2048], P(('seq', 'tp'))
- series_grad: bfloat16 [32768, 2048], P(('seq', 'tp'))
All inputs are finite; a program needn't handle non-finite values.
Results may differ from a plain program's by a relative error of at most 0.019.
Values may be sent and summed in bfloat16 or wider, within the bound.
No kernel may reach another device: no remote copies, remote signals or barrier semaphores. Data moves between devices by JAX's collectives and lax.ppermute only.
A program may use at most 128 MiB of HBM per device.

v0:
```python
import jax
import jax.numpy as jnp
from jax import lax
from jax.sharding import PartitionSpec as P

HD = 128
BLOCK = 64
NEG = -1e30
EPS = 1e-06


def shifted(value, axis, by):
    size = lax.axis_size(axis)
    pairs = [(i, i + by) for i in range(size) if 0 <= i + by < size]
    return lax.ppermute(value, axis, pairs)


def project_back(grads, weight):
    return jnp.einsum("tf,df->td", grads, weight, preferred_element_type=jnp.float32)


def per_device(series, norm_gain, w_query, w_key, w_value, w_out, out_grad):
    series_f = series.astype(jnp.float32)
    inv_rms = lax.rsqrt(jnp.mean(series_f * series_f, axis=-1, keepdims=True) + EPS)
    unit_rows = series_f * inv_rms
    normed_rows = (unit_rows * norm_gain).astype(jnp.bfloat16)
    gathered, out_grads = (
        lax.all_gather(normed_rows, "tp", axis=0, tiled=True),
        lax.all_gather(out_grad, "tp", axis=0, tiled=True),
    )
    tokens = gathered.shape[0]
    feat_width = w_query.shape[1]
    head_count = feat_width // HD
    blocks = tokens // BLOCK
    seq_devices = lax.axis_size("seq")
    levels = seq_devices.bit_length() - 1
    first_block = lax.axis_index("seq") * blocks
    factor = HD ** (-0.5)
    query_rows = jnp.dot(gathered, w_query, preferred_element_type=jnp.float32).astype(jnp.bfloat16)
    key_rows = jnp.dot(gathered, w_key, preferred_element_type=jnp.float32).astype(jnp.bfloat16)
    value_rows = jnp.dot(gathered, w_value, preferred_element_type=jnp.float32).astype(jnp.bfloat16)
    key_value = jnp.stack([key_rows, value_rows])
    fetched = [shifted(key_value, "seq", 2**section) for section in range(levels)]
    near_steps = [2**section for section in range(blocks.bit_length())]
    distances = near_steps + [blocks * 2**section for section in range(1, levels)]
    own_blocks = key_value.reshape(2, blocks, BLOCK, feat_width)
    extended = jnp.concatenate([fetched[0], key_value], axis=1).reshape(
        2, 2 * blocks, BLOCK, feat_width
    )
    pieces = [own_blocks] + [
        extended[:, blocks - distance : 2 * blocks - distance] for distance in near_steps
    ]
    pieces = pieces + [
        fetched[section].reshape(2, blocks, BLOCK, feat_width) for section in range(1, levels)
    ]
    keys_all = jnp.concatenate(pieces, axis=2)
    global_block = first_block + jnp.arange(blocks, dtype=jnp.int32)
    causal = lax.broadcasted_iota(jnp.int32, (BLOCK, BLOCK), 0) >= lax.broadcasted_iota(
        jnp.int32, (BLOCK, BLOCK), 1
    )
    mask_list = [jnp.broadcast_to(causal, (blocks, BLOCK, BLOCK))]
    mask_list = mask_list + [
        jnp.broadcast_to((global_block >= distance)[:, None, None], (blocks, BLOCK, BLOCK))
        for distance in distances
    ]
    key_mask = jnp.concatenate(mask_list, axis=2)[:, None]
    query_blocks = query_rows.reshape(blocks, BLOCK, head_count, HD)
    key_blocks = keys_all[0].reshape(blocks, -1, head_count, HD)
    value_blocks = keys_all[1].reshape(blocks, -1, head_count, HD)
    scores = (
        jnp.einsum("bqhe,bkhe->bhqk", query_blocks, key_blocks, preferred_element_type=jnp.float32)
        * factor
    )
    scores = jnp.where(key_mask, scores, NEG)
    peak_score = jnp.max(scores, axis=-1, keepdims=True)
    log_total = peak_score + jnp.log(jnp.sum(jnp.exp(scores - peak_score), axis=-1, keepdims=True))
    attn_prob = jnp.exp(scores - log_total)
    attn_weight = attn_prob.astype(jnp.bfloat16)
    mixed = jnp.einsum(
        "bhqk,bkhe->bqhe", attn_weight, value_blocks, preferred_element_type=jnp.float32
    ).astype(jnp.bfloat16)
    mixed_rows = mixed.reshape(tokens, feat_width)
    attn_rows = lax.psum_scatter(
        jnp.dot(mixed_rows, w_out, preferred_element_type=jnp.float32).astype(jnp.bfloat16),
        "tp",
        scatter_dimension=0,
        tiled=True,
    ).astype(jnp.float32)
    layer_out = (series_f + attn_rows).astype(jnp.bfloat16)
    grad_mixed = jnp.einsum(
        "td,fd->tf", out_grads, w_out, preferred_element_type=jnp.float32
    ).astype(jnp.bfloat16)
    grad_blocks = grad_mixed.reshape(blocks, BLOCK, head_count, HD)
    row_inner = jnp.einsum("bqhe,bqhe->bhq", grad_blocks, mixed, preferred_element_type=jnp.float32)
    grad_probs = jnp.einsum(
        "bqhe,bkhe->bhqk", grad_blocks, value_blocks, preferred_element_type=jnp.float32
    )
    grad_scores = (attn_prob * (grad_probs - row_inner[..., None])).astype(jnp.bfloat16)
    grad_query = (
        jnp.einsum("bhqk,bkhe->bqhe", grad_scores, key_blocks, preferred_element_type=jnp.float32)
        * factor
    ).astype(jnp.bfloat16)
    grad_query = grad_query.reshape(tokens, feat_width)
    grad_keys = (
        jnp.einsum("bhqk,bqhe->bkhe", grad_scores, query_blocks, preferred_element_type=jnp.float32)
        * factor
    )
    grad_values = jnp.einsum(
        "bhqk,bqhe->bkhe", attn_weight, grad_blocks, preferred_element_type=jnp.float32
    )
    grad_pairs = jnp.stack([grad_keys, grad_values]).reshape(2, blocks, -1, BLOCK, feat_width)
    spill_grads = jnp.zeros((2, 2 * blocks, BLOCK, feat_width), jnp.float32)
    for position, distance in enumerate(near_steps):
        spill_grads = spill_grads.at[:, blocks - distance : 2 * blocks - distance].add(
            grad_pairs[:, :, 1 + position]
        )
    own_grads = grad_pairs[:, :, 0] + spill_grads[:, blocks:]
    for section in range(levels):
        if section == 0:
            return_part = spill_grads[:, :blocks]
        else:
            return_part = grad_pairs[:, :, len(near_steps) + section]
        own_grads = own_grads + shifted(return_part, "seq", -(2**section))
    grad_key_rows = own_grads[0].reshape(tokens, feat_width).astype(jnp.bfloat16)
    grad_value_rows = own_grads[1].reshape(tokens, feat_width).astype(jnp.bfloat16)
    grad_normed = (
        project_back(grad_query, w_query)
        + project_back(grad_key_rows, w_key)
        + project_back(grad_value_rows, w_value)
    )
    grad_own = lax.psum_scatter(
        grad_normed.astype(jnp.bfloat16), "tp", scatter_dimension=0, tiled=True
    ).astype(jnp.float32)
    scaled = grad_own * norm_gain
    series_grad = out_grad.astype(jnp.float32) + inv_rms * (
        scaled - unit_rows * jnp.mean(scaled * unit_rows, axis=-1, keepdims=True)
    )
    return (layer_out, series_grad.astype(jnp.bfloat16))


def solution(mesh):
    in_specs = (
        P(("seq", "tp"), None),
        P(),
        P(None, "tp"),
        P(None, "tp"),
        P(None, "tp"),
        P("tp", None),
        P(("seq", "tp"), None),
    )
    out_specs = (P(("seq", "tp"), None), P(("seq", "tp"), None))
    return jax.shard_map(
        per_device, mesh=mesh, in_specs=in_specs, out_specs=out_specs, check_vma=False
    )
```

profile of v0, /device:TPU:1, one launch (start us, length us, event | category | flops | bytes accessed | tf_op | source)
XLA Modules:
  0.0 416.9 jit_solution(14355555327161746175)
XLA Ops:
  7.2 1.4 fusion.13
  8.6 2.0 fusion.7
  12.3 1.0 concatenate.19
  13.3 29.2 %all-gather.3.cloned.1.call-done = bf16[256,2048]{1,0:T(8,128)(2,1)} async-done(((bf16[128,2048]{1,0:T(8,128)(2,1)}), bf16[256,2048]{1,0:T(8,128)(2,1)}) %all-gather.3.cloned.1.call-update) | async-done | bytes 1048592 | tf_op jit(solution)/shard_map/all_gather | solution.py:28
  42.5 2.8 convolution_convert_fusion.4
  46.0 0.9 pad_maximum_fusion.1
  46.9 3.7 collective-permute-start
  50.6 3.2 collective-permute-start.1
  53.8 6.2 %collective-permute-start.2 = (bf16[2,256,512]{2,1,0:T(8,128)(2,1)}, bf16[2,256,512]{2,1,0:T(8,128)(2,1)}, u32[]{:S(2)}, u32[]{:S(2)}) collective-permute-start(bf16[2,256,512]{2,1,0:T(8,128)(2,1)} %pad_maximum_fusion.1), channel_id=1, source_target_pairs={{0,8},{2,10},{4,12},{6,14},{8,16},{10,18},{12,20},{14,22},{16,24},... | collective-permute-start | bytes 1572872 | tf_op jit(solution)/shard_map/ppermute | solution.py:15
  60.0 2.2 collective-permute-start.3
  62.2 3.7 collective-permute-start.4
  65.9 1.0 copy.23
  66.9 1.0 copy.22
  67.9 1.9 convolution_convert_fusion.3
  70.6 46.3 %all-gather.5.cloned.1.call-done = bf16[256,2048]{1,0:T(8,128)(2,1)} async-done(((bf16[128,2048]{1,0:T(8,128)(2,1)}), bf16[256,2048]{1,0:T(8,128)(2,1)}) %all-gather.5.cloned.1.call-update) | async-done | bytes 1048592 | tf_op jit(solution)/shard_map/all_gather | solution.py:29
  116.9 2.7 convolution_convert_fusion.2
  119.6 0.8 bitcast_convert_fusion
  120.5 3.9 collective-permute-start.5
  125.2 4.4 %collective-permute-start.6 = (bf16[2,256,512]{2,1,0:T(8,128)(2,1)}, bf16[2,256,512]{2,1,0:T(8,128)(2,1)}, u32[]{:S(2)}, u32[]{:S(2)}) collective-permute-start(bf16[2,256,512]{2,1,0:T(8,128)(2,1)} %pad_maximum_fusion.1), channel_id=1, source_target_pairs={{0,128},{2,130},{4,132},{6,134},{8,136},{10,138},{12,140},{14,142}... | collective-permute-start | bytes 1572872 | tf_op jit(solution)/shard_map/ppermute | solution.py:15
  129.5 1.4 pad_maximum_fusion
  131.0 1.1 maximum_maximum_fusion
  132.1 1.2 fusion.47
  133.3 2.4 copy.64
  135.7 2.3 copy.65
  138.0 2.5 copy.66
  140.5 2.4 copy.27
  142.9 2.4 copy.28
  145.3 2.4 copy.29
  147.6 2.4 copy.30
  150.0 2.4 copy.31
  152.4 2.4 copy.32
  154.8 12.3 %concatenate.18 = bf16[2,4,640,512]{2,3,1,0:T(8,128)(2,1)} concatenate(bf16[2,4,64,512]{2,3,1,0:T(8,128)(2,1)S(1)} %pad_maximum_fusion, bf16[2,4,64,512]{2,3,1,0:T(8,128)(2,1)} %copy.64, bf16[2,4,64,512]{2,3,1,0:T(8,128)(2,1)} %copy.65, bf16[2,4,64,512]{2,3,1,0:T(8,128)(2,1)} %copy.66, bf16[2,4,64,512]{2,3,1,0:T(8,128)(2,1)} %copy.27, bf16[2,4,64,512]{2,3,1,0:T(8,128)(2,1)} %copy.28, ...), dimensions={2} | concatenate | bytes 10485760 | tf_op jit(solution)/shard_map/concatenate | solution.py:56
  167.1 3.0 fusion.46
  172.5 3.2 convolution_bitcast_fusion
  175.7 2.0 multiply_reduce_fusion
  178.5 3.3 multiply_bitcast_fusion
  181.8 7.2 %copy.42 = f32[4,640,4,128]{3,2,1,0:T(4,128)} copy(f32[4,640,4,128]{1,3,2,0:T(8,128)} %multiply_bitcast_fusion) | data formatting | bytes 10485760 | tf_op jit(solution)/shard_map/mul | solution.py:105
  189.0 7.4 %stack.30 = f32[1,4,10,64,512]{4,3,2,1,0:T(8,128)} reshape(f32[4,640,4,128]{3,2,1,0:T(4,128)} %copy.42) | data formatting | bytes 10485760 | tf_op jit(solution)/shard_map/stack | solution.py:111
  196.4 5.8 %constant_dynamic-update-slice_fusion.1 = f32[2,4,10,64,512]{4,3,2,1,0:T(8,128)} fusion(f32[1,4,10,64,512]{4,3,2,1,0:T(8,128)} %stack.30), kind=kLoop, calls=%fused_computation.73 | loop fusion | bytes 10485760
  202.2 7.2 %copy.44 = f32[4,640,4,128]{3,2,1,0:T(4,128)} copy(f32[4,640,4,128]{1,3,2,0:T(8,128)} %convolution_bitcast_fusion) | data formatting | bytes 10485760 | tf_op jit(solution)/shard_map/bhqk,bqhe->bkhe/transpose | solution.py:108
  209.4 7.4 %stack.31 = f32[1,4,10,64,512]{4,3,2,1,0:T(8,128)} reshape(f32[4,640,4,128]{3,2,1,0:T(4,128)} %copy.44) | data formatting | bytes 10485760 | tf_op jit(solution)/shard_map/stack | solution.py:111
  216.9 5.9 %constant_dynamic-update-slice_fusion = f32[2,4,10,64,512]{4,3,2,1,0:T(8,128)} fusion(f32[2,4,10,64,512]{4,3,2,1,0:T(8,128)} %constant_dynamic-update-slice_fusion.1, f32[1,4,10,64,512]{4,3,2,1,0:T(8,128)} %stack.31), kind=kLoop, calls=%fused_computation.72 | loop fusion | bytes 10485760 | tf_op jit(solution)/shard_map/stack | solution.py:111
  222.7 4.6 %slice_bitcast_fusion.8 = (f32[2,4,64,512]{3,2,1,0:T(8,128)S(1)}, f32[2,4,64,512]{3,2,1,0:T(8,128)S(1)}, f32[2,4,64,512]{3,2,1,0:T(8,128)S(1)}, f32[2,4,64,512]{...) fusion(f32[2,4,10,64,512]{4,3,2,1,0:T(8,128)} %constant_dynamic, ...), kind=kLoop, calls=%fused_computation.53 | loop fusion | bytes 14680064 | tf_op jit(solution)/shard_map/add | solution.py:114
  227.4 1.3 collective-permute-start.13
  228.7 1.3 collective-permute-start.12
  230.0 1.3 collective-permute-start.11
  231.3 1.3 collective-permute-start.10
  232.6 1.3 collective-permute-start.9
  234.1 1.7 fusion.25
  235.8 1.4 fusion.15
  237.2 17.2 %collective-permute-done.13 = f32[2,4,64,512]{3,2,1,0:T(8,128)S(1)} collective-permute-done((f32[2,4,64,512]{3,2,1,0:T(8,128)S(1)}, f32[2,4,64,512]{3,2,1,0:T(8,128)S(1)}, u32[]{:S(2)}, u32[]{:S(2)}) %collective-permute-start.13) | collective-permute-done | bytes 1048608 | tf_op jit(solution)/shard_map/ppermute | solution.py:15
  254.4 1.3 collective-permute-start.8
  255.7 4.1 collective-permute-start.7
  259.8 1.2 fusion.6
  262.0 19.3 %collective-permute-done.9 = f32[2,4,64,512]{3,2,1,0:T(8,128)S(1)} collective-permute-done((f32[2,4,64,512]{3,2,1,0:T(8,128)S(1)}, f32[2,4,64,512]{3,2,1,0:T(8,128)S(1)}, u32[]{:S(2)}, u32[]{:S(2)}) %collective-permute-start.9) | collective-permute-done | bytes 1048608 | tf_op jit(solution)/shard_map/ppermute | solution.py:15
  281.3 21.0 %collective-permute-done.8 = f32[2,4,64,512]{3,2,1,0:T(8,128)S(1)} collective-permute-done((f32[2,4,64,512]{3,2,1,0:T(8,128)S(1)}, f32[2,4,64,512]{3,2,1,0:T(8,128)S(1)}, u32[]{:S(2)}, u32[]{:S(2)}) %collective-permute-start.8) | collective-permute-done | bytes 1048608 | tf_op jit(solution)/shard_map/ppermute | solution.py:15
  302.3 11.8 %collective-permute-done.7 = f32[2,4,64,512]{3,2,1,0:T(8,128)S(1)} collective-permute-done((f32[2,4,64,512]{3,2,1,0:T(8,128)S(1)}, f32[2,4,64,512]{3,2,1,0:T(8,128)S(1)}, u32[]{:S(2)}, u32[]{:S(2)}) %collective-permute-start.7) | collective-permute-done | bytes 1048608 | tf_op jit(solution)/shard_map/ppermute | solution.py:15
  314.1 2.2 fusion.23
  318.0 1.7 fusion
  320.0 3.3 convolution_convert_fusion
  323.4 55.4 %reduce-scatter.5.cloned.1.call-done = bf16[128,2048]{1,0:T(8,128)(2,1)} async-done(((bf16[256,2048]{1,0:T(8,128)(2,1)}), bf16[128,2048]{1,0:T(8,128)(2,1)}) %reduce-scatter.5.cloned.1.call-update) | async-done | bytes 524304 | tf_op jit(solution)/shard_map/reduce_scatter | solution.py:131
  378.8 1.4 fusion.8
  380.2 27.5 %reduce-scatter.3.cloned.1.call-done = bf16[128,2048]{1,0:T(8,128)(2,1)} async-done(((bf16[256,2048]{1,0:T(8,128)(2,1)}), bf16[128,2048]{1,0:T(8,128)(2,1)}) %reduce-scatter.3.cloned.1.call-update) | async-done | bytes 524304 | tf_op jit(solution)/shard_map/reduce_scatter | solution.py:83
  407.7 2.7 fusion.12
  (91 shorter events, 10.2 us)
Async XLA Ops:
  7.2 60.7 %copy-start = (bf16[2048,512]{1,0:T(8,128)(2,1)S(1)}, bf16[2048,512]{1,0:T(8,128)(2,1)}, u32[]{:S(2)}) copy-start(bf16[2048,512]{1,0:T(8,128)(2,1)} %param.15) | copy-start | bytes 6291460
  7.2 35.3 %all-gather.3.cloned.1.call-start = ((), (), s32[]{:S(2)}) async-start(), calls=%async_computation.2 | async-start | bytes 1572864 | tf_op jit(solution)/shard_map/all_gather | solution.py:28
  10.7 106.2 %all-gather.5.cloned.1.call-start = ((), (), s32[]{:S(2)}) async-start(), calls=%async_computation.4 | async-start | bytes 1572864 | tf_op jit(solution)/shard_map/all_gather | solution.py:29
  11.4 367.4 %reduce-scatter.5.cloned.1.call-start = ((), (), s32[]{:S(2)}) async-start(), calls=%async_computation.5 | async-start | bytes 1572864 | tf_op jit(solution)/shard_map/reduce_scatter | solution.py:131
  42.5 2.8 copy-start.11
  42.5 2.8 copy-start.20
  45.3 21.6 %copy-start.7 = (bf16[256,512]{1,0:T(8,128)(2,1)}, bf16[256,512]{1,0:T(8,128)(2,1)S(1)}, u32[]{:S(2)}) copy-start(bf16[256,512]{1,0:T(8,128)(2,1)S(1)} %convolution_convert_fusion.4) | copy-start | bytes 786436
  46.0 23.8 %copy-start.9 = (bf16[256,512]{1,0:T(8,128)(2,1)}, bf16[256,512]{1,0:T(8,128)(2,1)S(1)}, u32[]{:S(2)}) copy-start(bf16[256,512]{1,0:T(8,128)(2,1)S(1)} %convolution_convert_fusion.5) | copy-start | bytes 786436
  46.9 73.6 %collective-permute-start = (bf16[2,256,512]{2,1,0:T(8,128)(2,1)}, bf16[2,256,512]{2,1,0:T(8,128)(2,1)}, u32[]{:S(2)}, u32[]{:S(2)}) collective-permute-start(bf16[2,256,512]{2,1,0:T(8,128)(2,1)} %pad_maximum_fusion.1), channel_id=1, source_target_pairs={{0,2},{2,4},{4,6},{6,8},{8,10},{10,12},{12,14},{14,16},{16,18},{18... | collective-permute-start | bytes 1572872 | tf_op jit(solution)/shard_map/ppermute | solution.py:15
  50.6 73.8 %collective-permute-start.1 = (bf16[2,256,512]{2,1,0:T(8,128)(2,1)}, bf16[2,256,512]{2,1,0:T(8,128)(2,1)S(1)}, u32[]{:S(2)}, u32[]{:S(2)}) collective-permute-start(bf16[2,256,512]{2,1,0:T(8,128)(2,1)} %pad_maximum_fusion.1), channel_id=1, source_target_pairs={{0,4},{2,6},{4,8},{6,10},{8,12},{10,14},{12,16},{14,18},{16,20},{1... | collective-permute-start | bytes 1572872 | tf_op jit(solution)/shard_map/ppermute | solution.py:15
  53.8 89.1 %collective-permute-start.2 = (bf16[2,256,512]{2,1,0:T(8,128)(2,1)}, bf16[2,256,512]{2,1,0:T(8,128)(2,1)}, u32[]{:S(2)}, u32[]{:S(2)}) collective-permute-start(bf16[2,256,512]{2,1,0:T(8,128)(2,1)} %pad_maximum_fusion.1), channel_id=1, source_target_pairs={{0,8},{2,10},{4,12},{6,14},{8,16},{10,18},{12,20},{14,22},{16,24},... | collective-permute-start | bytes 1572872 | tf_op jit(solution)/shard_map/ppermute | solution.py:15
  60.0 85.3 %collective-permute-start.3 = (bf16[2,256,512]{2,1,0:T(8,128)(2,1)}, bf16[2,256,512]{2,1,0:T(8,128)(2,1)}, u32[]{:S(2)}, u32[]{:S(2)}) collective-permute-start(bf16[2,256,512]{2,1,0:T(8,128)(2,1)} %pad_maximum_fusion.1), channel_id=1, source_target_pairs={{0,16},{2,18},{4,20},{6,22},{8,24},{10,26},{12,28},{14,30},{16,32}... | collective-permute-start | bytes 1572872 | tf_op jit(solution)/shard_map/ppermute | solution.py:15
  62.2 85.5 %collective-permute-start.4 = (bf16[2,256,512]{2,1,0:T(8,128)(2,1)}, bf16[2,256,512]{2,1,0:T(8,128)(2,1)}, u32[]{:S(2)}, u32[]{:S(2)}) collective-permute-start(bf16[2,256,512]{2,1,0:T(8,128)(2,1)} %pad_maximum_fusion.1), channel_id=1, source_target_pairs={{0,32},{2,34},{4,36},{6,38},{8,40},{10,42},{12,44},{14,46},{16,48}... | collective-permute-start | bytes 1572872 | tf_op jit(solution)/shard_map/ppermute | solution.py:15
  119.6 52.9 %copy-start.4 = (bf16[4,64,4,128]{3,2,1,0:T(4,128)(2,1)}, bf16[4,64,4,128]{3,2,1,0:T(4,128)(2,1)S(1)}, u32[]{:S(2)}) copy-start(bf16[4,64,4,128]{3,2,1,0:T(4,128)(2,1)S(1)} %reshape.218) | copy-start | bytes 786436
  119.6 11.4 %copy-start.8 = (bf16[256,512]{1,0:T(8,128)(2,1)S(1)}, bf16[256,512]{1,0:T(8,128)(2,1)}, u32[]{:S(2)}) copy-start(bf16[256,512]{1,0:T(8,128)(2,1)} %copy-done.7) | copy-start | bytes 786436
  119.6 11.4 %copy-start.10 = (bf16[256,512]{1,0:T(8,128)(2,1)S(1)}, bf16[256,512]{1,0:T(8,128)(2,1)}, u32[]{:S(2)}) copy-start(bf16[256,512]{1,0:T(8,128)(2,1)} %copy-done.9) | copy-start | bytes 786436
  120.5 29.6 %collective-permute-start.5 = (bf16[2,256,512]{2,1,0:T(8,128)(2,1)}, bf16[2,256,512]{2,1,0:T(8,128)(2,1)}, u32[]{:S(2)}, u32[]{:S(2)}) collective-permute-start(bf16[2,256,512]{2,1,0:T(8,128)(2,1)} %pad_maximum_fusion.1), channel_id=1, source_target_pairs={{0,64},{2,66},{4,68},{6,70},{8,72},{10,74},{12,76},{14,78},{16,80}... | collective-permute-start | bytes 1572872 | tf_op jit(solution)/shard_map/ppermute | solution.py:15
  124.4 0.8 copy-start.18
  125.2 27.2 %collective-permute-start.6 = (bf16[2,256,512]{2,1,0:T(8,128)(2,1)}, bf16[2,256,512]{2,1,0:T(8,128)(2,1)}, u32[]{:S(2)}, u32[]{:S(2)}) collective-permute-start(bf16[2,256,512]{2,1,0:T(8,128)(2,1)} %pad_maximum_fusion.1), channel_id=1, source_target_pairs={{0,128},{2,130},{4,132},{6,134},{8,136},{10,138},{12,140},{14,142}... | collective-permute-start | bytes 1572872 | tf_op jit(solution)/shard_map/ppermute | solution.py:15
  167.1 3.1 copy-start.6
  167.1 3.1 copy-start.17
  170.2 1.5 copy-start.1
  172.5 3.3 copy-start.13
  175.7 2.0 copy-start.5
  227.4 27.0 %collective-permute-start.13 = (f32[2,4,64,512]{3,2,1,0:T(8,128)S(1)}, f32[2,4,64,512]{3,2,1,0:T(8,128)S(1)}, u32[]{:S(2)}, u32[]{:S(2)}) collective-permute-start(f32[2,4,64,512]{3,2,1,0:T(8,128)S(1)} %get-tuple-element.43), channel_id=1, source_target_pairs={{128,0},{130,2},{132,4},{134,6},{136,8},{138,10},{140,12},{142,14}... | collective-permute-start | bytes 3145736 | tf_op jit(solution)/shard_map/ppermute | solution.py:15
  228.7 27.0 %collective-permute-start.12 = (f32[2,4,64,512]{3,2,1,0:T(8,128)S(1)}, f32[2,4,64,512]{3,2,1,0:T(8,128)S(1)}, u32[]{:S(2)}, u32[]{:S(2)}) collective-permute-start(f32[2,4,64,512]{3,2,1,0:T(8,128)S(1)} %get-tuple-element.44), channel_id=1, source_target_pairs={{64,0},{66,2},{68,4},{70,6},{72,8},{74,10},{76,12},{78,14},{80,16}... | collective-permute-start | bytes 3145736 | tf_op jit(solution)/shard_map/ppermute | solution.py:15
  230.0 32.0 %collective-permute-start.11 = (f32[2,4,64,512]{3,2,1,0:T(8,128)S(1)}, f32[2,4,64,512]{3,2,1,0:T(8,128)S(1)}, u32[]{:S(2)}, u32[]{:S(2)}) collective-permute-start(f32[2,4,64,512]{3,2,1,0:T(8,128)S(1)} %get-tuple-element.39), channel_id=1, source_target_pairs={{32,0},{34,2},{36,4},{38,6},{40,8},{42,10},{44,12},{46,14},{48,16}... | collective-permute-start | bytes 3145736 | tf_op jit(solution)/shard_map/ppermute | solution.py:15
  231.3 30.7 %collective-permute-start.10 = (f32[2,4,64,512]{3,2,1,0:T(8,128)S(1)}, f32[2,4,64,512]{3,2,1,0:T(8,128)S(1)}, u32[]{:S(2)}, u32[]{:S(2)}) collective-permute-start(f32[2,4,64,512]{3,2,1,0:T(8,128)S(1)} %get-tuple-element.40), channel_id=1, source_target_pairs={{16,0},{18,2},{20,4},{22,6},{24,8},{26,10},{28,12},{30,14},{32,16}... | collective-permute-start | bytes 3145736 | tf_op jit(solution)/shard_map/ppermute | solution.py:15
  232.6 48.7 %collective-permute-start.9 = (f32[2,4,64,512]{3,2,1,0:T(8,128)S(1)}, f32[2,4,64,512]{3,2,1,0:T(8,128)S(1)}, u32[]{:S(2)}, u32[]{:S(2)}) collective-permute-start(f32[2,4,64,512]{3,2,1,0:T(8,128)S(1)} %get-tuple-element.41), channel_id=1, source_target_pairs={{8,0},{10,2},{12,4},{14,6},{16,8},{18,10},{20,12},{22,14},{24,16},... | collective-permute-start | bytes 3145736 | tf_op jit(solution)/shard_map/ppermute | solution.py:15
  234.1 25.7 %copy-start.2 = (bf16[1,4,640,512]{2,3,1,0:T(8,128)(2,1)S(1)}, bf16[1,4,640,512]{2,3,1,0:T(8,128)(2,1)}, u32[]{:S(2)}) copy-start(bf16[1,4,640,512]{2,3,1,0:T(8,128)(2,1)} %copy-done.1) | copy-start | bytes 7864324
  254.4 47.9 %collective-permute-start.8 = (f32[2,4,64,512]{3,2,1,0:T(8,128)S(1)}, f32[2,4,64,512]{3,2,1,0:T(8,128)S(1)}, u32[]{:S(2)}, u32[]{:S(2)}) collective-permute-start(f32[2,4,64,512]{3,2,1,0:T(8,128)S(1)} %get-tuple-element.42), channel_id=1, source_target_pairs={{4,0},{6,2},{8,4},{10,6},{12,8},{14,10},{16,12},{18,14},{20,16},{2... | collective-permute-start | bytes 3145736 | tf_op jit(solution)/shard_map/ppermute | solution.py:15
  255.7 58.4 %collective-permute-start.7 = (f32[2,4,64,512]{3,2,1,0:T(8,128)S(1)}, f32[2,4,64,512]{3,2,1,0:T(8,128)S(1)}, u32[]{:S(2)}, u32[]{:S(2)}) collective-permute-start(f32[2,4,64,512]{3,2,1,0:T(8,128)S(1)} %fusion.15), channel_id=1, source_target_pairs={{2,0},{4,2},{6,4},{8,6},{10,8},{12,10},{14,12},{16,14},{18,16},{20... | collective-permute-start | bytes 3145736 | tf_op jit(solution)/shard_map/ppermute | solution.py:15
  261.9 54.4 %copy-start.12 = (bf16[2048,512]{1,0:T(8,128)(2,1)S(1)}, bf16[2048,512]{1,0:T(8,128)(2,1)}, u32[]{:S(2)}) copy-start(bf16[2048,512]{1,0:T(8,128)(2,1)} %param.16) | copy-start | bytes 6291460
  316.4 1.6 copy-start.14
  318.0 1.8 copy-start.16
  319.7 59.1 %copy-start.3 = (bf16[128,2048]{1,0:T(8,128)(2,1)S(1)}, bf16[128,2048]{1,0:T(8,128)(2,1)}, u32[]{:S(2)}) copy-start(bf16[128,2048]{1,0:T(8,128)(2,1)} %param.13) | copy-start | bytes 1572868
  319.7 59.1 %copy-start.19 = (f32[2048]{0:T(1024)S(1)}, f32[2048]{0:T(1024)}, u32[]{:S(2)}) copy-start(f32[2048]{0:T(1024)} %param.14) | copy-start | bytes 24580
  319.7 88.0 %reduce-scatter.3.cloned.1.call-start = ((), (), s32[]{:S(2)}) async-start(), calls=%async_computation.3 | async-start | bytes 1572864 | tf_op jit(solution)/shard_map/reduce_scatter | solution.py:83
  320.0 87.7 %copy-start.15 = (bf16[128,2048]{1,0:T(8,128)(2,1)S(1)}, bf16[128,2048]{1,0:T(8,128)(2,1)}, u32[]{:S(2)}) copy-start(bf16[128,2048]{1,0:T(8,128)(2,1)} %param.19) | copy-start | bytes 1572868
Sparse Core Ops, SparseCore 0:
  10.8 31.6 all-gather.2
  44.3 72.5 all-gather.4
  319.8 58.9 reduce-scatter.4
  381.3 26.3 reduce-scatter.2
where the time goes:
time: 420 us; the launch traced here: 417 us
  waiting for transfers between devices  228 us (54%)
  local copies, waits for them, and re-layouts  91.2 us (22%)
  starting transfers between devices  39.2 us (9%)
  matrix products  25.9 us (6%)
  other arithmetic  17.9 us (4%)
  between operations  14.3 us (3%)
    ppermute x14, waiting for transfers between devices, shifted(): return lax.ppermute(value, axis, pairs)  69.3 us
    reduce_scatter x1, waiting for transfers between devices, per_device(): lax.psum_scatter(grad_normed.astype(jnp.bfloat16), 'tp', scatter_dimensio...  55.4 us
    all_gather x1, waiting for transfers between devices, per_device(): lax.all_gather(out_grad, 'tp', axis=0, tiled=True)  46.3 us
    ppermute x14, starting transfers between devices, shifted(): return lax.ppermute(value, axis, pairs)  39.1 us
    all_gather x1, waiting for transfers between devices, per_device(): lax.all_gather(normed_rows, 'tp', axis=0, tiled=True)  29.2 us
    reduce_scatter x1, waiting for transfers between devices, per_device(): lax.psum_scatter(jnp.dot(mixed_rows, w_out, preferred_element_type=jnp.fl...  27.5 us
    another operation x3, local copies, waits for them, and re-layouts, per_device(): jnp.stack([grad_keys, grad_values])  20.7 us
    unnamed x46, local copies, waits for them, and re-layouts  15.4 us
  transfers between devices with their start and end apart: 18, of which 8 were waited for; matrix products, arithmetic and copies ran while one was open for 11% of the time, Pallas kernels for 0%

commit v1 on v0

--- a/solution.py
+++ b/solution.py
@@ -7,6 +7,19 @@
 BLOCK = 64
 NEG = -1e30
 EPS = 1e-06
+
+
+def chains_answer(obj, row_axis):
+    y = jnp.concatenate(
+        lax.all_to_all(
+            jnp.stack(lax.axis_size(row_axis) * [obj], axis=0),
+            axis_name=row_axis,
+            split_axis=0,
+            concat_axis=0,
+        ),
+        0,
+    )
+    return y
 
 
 def shifted(value, axis, by):
@@ -26,7 +39,7 @@
     normed_rows = (unit_rows * norm_gain).astype(jnp.bfloat16)
     gathered, out_grads = (
         lax.all_gather(normed_rows, "tp", axis=0, tiled=True),
-        lax.all_gather(out_grad, "tp", axis=0, tiled=True),
+        chains_answer(out_grad, "tp"),
     )
     tokens = gathered.shape[0]
     feat_width = w_query.shape[1]

time: 420 us -> 424 us (level)
  starting transfers between devices: 39.2 us -> 49.4 us
  waiting for transfers between devices: 228 us -> 220 us
    all_gather x1 -> x0, waiting for transfers between devices: 46.3 us -> none  [per_device(): lax.all_gather(out_grad, 'tp', axis=0, tiled=True)]
    reduce_scatter x1, waiting for transfers between devices: 55.4 us -> 81.7 us  [per_device(): lax.psum_scatter(grad_normed.astype(jnp.bfloat16), 'tp', scatter_dimensio...]
    ppermute x14, waiting for transfers between devices: 69.3 us -> 87.9 us  [shifted(): return lax.ppermute(value, axis, pairs)]
    all_gather x1, waiting for transfers between devices: 29.2 us -> 11.5 us  [per_device(): lax.all_gather(normed_rows, 'tp', axis=0, tiled=True)]
    all_to_all x0 -> x1, waiting for transfers between devices: none -> 11.3 us  [chains_answer(): lax.all_to_all(jnp.stack(lax.axis_size(row_axis) * [obj], axis=0), axis_n...]
    ppermute x14, starting transfers between devices: 39.1 us -> 44.5 us  [shifted(): return lax.ppermute(value, axis, pairs)]
    all_to_all x0 -> x1, starting transfers between devices: none -> 4.84 us  [chains_answer(): lax.all_to_all(jnp.stack(lax.axis_size(row_axis) * [obj], axis=0), axis_n...]
    unnamed x46 -> x42, local copies, waits for them, and re-layouts: 15.4 us -> 15.4 us
  transfers between devices with their start and end apart: 18 -> 18, of which waited for: 8 -> 13; matrix products, arithmetic and copies ran while one was open for 11% -> 11% of each run, Pallas kernels for 0% -> 0%
where the time goes in v1:
time: 424 us; the launch traced here: 421 us
  waiting for transfers between devices  220 us (52%)
  local copies, waits for them, and re-layouts  91.3 us (22%)
  starting transfers between devices  49.4 us (12%)
  matrix products  25.5 us (6%)
  other arithmetic  20.4 us (5%)
  between operations  14.2 us (3%)
    ppermute x14, waiting for transfers between devices, shifted(): return lax.ppermute(value, axis, pairs)  87.9 us
    reduce_scatter x1, waiting for transfers between devices, per_device(): lax.psum_scatter(grad_normed.astype(jnp.bfloat16), 'tp', scatter_dimensio...  81.7 us
    ppermute x14, starting transfers between devices, shifted(): return lax.ppermute(value, axis, pairs)  44.5 us
    reduce_scatter x1, waiting for transfers between devices, per_device(): lax.psum_scatter(jnp.dot(mixed_rows, w_out, preferred_element_type=jnp.fl...  27.7 us
    another operation x3, local copies, waits for them, and re-layouts, per_device(): jnp.stack([grad_keys, grad_values])  20.7 us
    unnamed x42, local copies, waits for them, and re-layouts  15.4 us
    reshape x6, local copies, waits for them, and re-layouts, per_device(): fetched[section].reshape(2, blocks, BLOCK, feat_width)  14.3 us
    concatenate x1, local copies, waits for them, and re-layouts, per_device(): keys_all = jnp.concatenate(pieces, axis=2)  12.3 us
  transfers between devices with their start and end apart: 18, of which 13 were waited for; matrix products, arithmetic and copies ran while one was open for 11% of the time, Pallas kernels for 0%

profile of v1, /device:TPU:1, one launch (start us, length us, event | category | flops | bytes accessed | tf_op | source)
XLA Modules:
  0.0 421.0 jit_solution(7806891646676001152)
XLA Ops:
  7.2 1.4 fusion.13
  8.6 2.0 fusion.7
  10.7 2.3 pad_maximum_fusion.1
  13.0 4.8 %all-to-all-start = ((bf16[2,128,2048]{2,1,0:T(8,128)(2,1)}), bf16[2,128,2048]{2,1,0:T(8,128)(2,1)S(1)}, u32[]{:S(2)}, u32[]{:S(2)}) async-start(bf16[2,128,2048]{2,1,0:T(8,128)(2,1)} %pad_maximum_fusion.1), calls=%async_computation.1 | async-start | bytes 2097152 | tf_op jit(solution)/shard_map/all_to_all | solution.py:14
  18.7 1.0 concatenate.19
  19.7 11.3 %all-to-all-done = bf16[2,128,2048]{2,1,0:T(8,128)(2,1)S(1)} async-done(((bf16[2,128,2048]{2,1,0:T(8,128)(2,1)}), bf16[2,128,2048]{2,1,0:T(8,128)(2,1)S(1)}, u32[]{:S(2)}, u32[]{:S(2)}) %all-to-all-start) | async-done | bytes 1048608 | tf_op jit(solution)/shard_map/all_to_all | solution.py:14
  31.0 2.3 convolution_convert_fusion.2
  33.4 11.5 %all-gather.2.cloned.1.call-done = bf16[256,2048]{1,0:T(8,128)(2,1)} async-done(((bf16[128,2048]{1,0:T(8,128)(2,1)}), bf16[256,2048]{1,0:T(8,128)(2,1)}) %all-gather.2.cloned.1.call-update) | async-done | bytes 1048592 | tf_op jit(solution)/shard_map/all_gather | solution.py:41
  44.9 2.8 convolution_convert_fusion.4
  49.3 3.9 collective-permute-start
  53.2 3.6 collective-permute-start.1
  57.6 6.9 %collective-permute-start.2 = (bf16[2,256,512]{2,1,0:T(8,128)(2,1)}, bf16[2,256,512]{2,1,0:T(8,128)(2,1)}, u32[]{:S(2)}, u32[]{:S(2)}) collective-permute-start(bf16[2,256,512]{2,1,0:T(8,128)(2,1)} %pad_maximum_fusion.2), channel_id=1, source_target_pairs={{0,8},{2,10},{4,12},{6,14},{8,16},{10,18},{12,20},{14,22},{16,24},... | collective-permute-start | bytes 1572872 | tf_op jit(solution)/shard_map/ppermute | solution.py:28
  64.5 3.3 collective-permute-start.3
  67.7 2.7 collective-permute-start.4
  72.5 1.9 convolution_convert_fusion.3
  75.2 3.2 collective-permute-start.5
  79.2 8.1 %collective-permute-start.6 = (bf16[2,256,512]{2,1,0:T(8,128)(2,1)}, bf16[2,256,512]{2,1,0:T(8,128)(2,1)}, u32[]{:S(2)}, u32[]{:S(2)}) collective-permute-start(bf16[2,256,512]{2,1,0:T(8,128)(2,1)} %pad_maximum_fusion.2), channel_id=1, source_target_pairs={{0,128},{2,130},{4,132},{6,134},{8,136},{10,138},{12,140},{14,142}... | collective-permute-start | bytes 1572872 | tf_op jit(solution)/shard_map/ppermute | solution.py:28
  87.3 1.4 pad_maximum_fusion
  88.8 1.3 maximum_maximum_fusion
  90.1 1.2 fusion.47
  91.2 2.4 copy.64
  93.6 2.3 copy.65
  96.0 2.5 copy.66
  98.4 2.4 copy.27
  100.8 2.4 copy.28
  103.2 2.4 copy.29
  105.6 1.8 collective-permute-done.4
  107.4 2.4 copy.30
  109.8 9.8 %collective-permute-done.5 = bf16[2,256,512]{2,1,0:T(8,128)(2,1)} collective-permute-done((bf16[2,256,512]{2,1,0:T(8,128)(2,1)}, bf16[2,256,512]{2,1,0:T(8,128)(2,1)}, u32[]{:S(2)}, u32[]{:S(2)}) %collective-permute-start.5) | collective-permute-done | bytes 524320 | tf_op jit(solution)/shard_map/ppermute | solution.py:28
  119.6 2.4 copy.31
  122.0 8.9 %collective-permute-done.6 = bf16[2,256,512]{2,1,0:T(8,128)(2,1)} collective-permute-done((bf16[2,256,512]{2,1,0:T(8,128)(2,1)}, bf16[2,256,512]{2,1,0:T(8,128)(2,1)}, u32[]{:S(2)}, u32[]{:S(2)}) %collective-permute-start.6) | collective-permute-done | bytes 524320 | tf_op jit(solution)/shard_map/ppermute | solution.py:28
  130.9 2.4 copy.32
  133.2 12.3 %concatenate.18 = bf16[2,4,640,512]{2,3,1,0:T(8,128)(2,1)} concatenate(bf16[2,4,64,512]{2,3,1,0:T(8,128)(2,1)S(1)} %pad_maximum_fusion, bf16[2,4,64,512]{2,3,1,0:T(8,128)(2,1)} %copy.64, bf16[2,4,64,512]{2,3,1,0:T(8,128)(2,1)} %copy.65, bf16[2,4,64,512]{2,3,1,0:T(8,128)(2,1)} %copy.66, bf16[2,4,64,512]{2,3,1,0:T(8,128)(2,1)} %copy.27, bf16[2,4,64,512]{2,3,1,0:T(8,128)(2,1)} %copy.28, ...), dimensions={2} | concatenate | bytes 10485760 | tf_op jit(solution)/shard_map/concatenate | solution.py:69
  145.6 3.0 fusion.46
  150.9 3.2 convolution_bitcast_fusion
  154.2 2.0 multiply_reduce_fusion
  156.9 3.3 multiply_bitcast_fusion
  160.2 7.2 %copy.42 = f32[4,640,4,128]{3,2,1,0:T(4,128)} copy(f32[4,640,4,128]{1,3,2,0:T(8,128)} %multiply_bitcast_fusion) | data formatting | bytes 10485760 | tf_op jit(solution)/shard_map/mul | solution.py:118
  167.4 7.4 %stack.39 = f32[1,4,10,64,512]{4,3,2,1,0:T(8,128)} reshape(f32[4,640,4,128]{3,2,1,0:T(4,128)} %copy.42) | data formatting | bytes 10485760 | tf_op jit(solution)/shard_map/stack | solution.py:124
  174.9 5.8 %constant_dynamic-update-slice_fusion.1 = f32[2,4,10,64,512]{4,3,2,1,0:T(8,128)} fusion(f32[1,4,10,64,512]{4,3,2,1,0:T(8,128)} %stack.39), kind=kLoop, calls=%fused_computation.74 | loop fusion | bytes 10485760
  180.7 7.2 %copy.44 = f32[4,640,4,128]{3,2,1,0:T(4,128)} copy(f32[4,640,4,128]{1,3,2,0:T(8,128)} %convolution_bitcast_fusion) | data formatting | bytes 10485760 | tf_op jit(solution)/shard_map/bhqk,bqhe->bkhe/transpose | solution.py:121
  187.9 7.4 %stack.40 = f32[1,4,10,64,512]{4,3,2,1,0:T(8,128)} reshape(f32[4,640,4,128]{3,2,1,0:T(4,128)} %copy.44) | data formatting | bytes 10485760 | tf_op jit(solution)/shard_map/stack | solution.py:124
  195.3 5.9 %constant_dynamic-update-slice_fusion = f32[2,4,10,64,512]{4,3,2,1,0:T(8,128)} fusion(f32[2,4,10,64,512]{4,3,2,1,0:T(8,128)} %constant_dynamic-update-slice_fusion.1, f32[1,4,10,64,512]{4,3,2,1,0:T(8,128)} %stack.40), kind=kLoop, calls=%fused_computation.73 | loop fusion | bytes 10485760 | tf_op jit(solution)/shard_map/stack | solution.py:124
  201.2 4.6 %slice_bitcast_fusion.8 = (f32[2,4,64,512]{3,2,1,0:T(8,128)S(1)}, f32[2,4,64,512]{3,2,1,0:T(8,128)S(1)}, f32[2,4,64,512]{3,2,1,0:T(8,128)S(1)}, f32[2,4,64,512]{...) fusion(f32[2,4,10,64,512]{4,3,2,1,0:T(8,128)} %constant_dynamic, ...), kind=kLoop, calls=%fused_computation.53 | loop fusion | bytes 14680064 | tf_op jit(solution)/shard_map/add | solution.py:127
  205.8 1.3 collective-permute-start.13
  207.1 1.3 collective-permute-start.12
  208.4 1.3 collective-permute-start.11
  209.7 1.3 collective-permute-start.10
  211.0 1.3 collective-permute-start.9
  212.6 1.7 fusion.25
  214.3 1.4 fusion.15
  215.7 15.6 %collective-permute-done.13 = f32[2,4,64,512]{3,2,1,0:T(8,128)S(1)} collective-permute-done((f32[2,4,64,512]{3,2,1,0:T(8,128)S(1)}, f32[2,4,64,512]{3,2,1,0:T(8,128)S(1)}, u32[]{:S(2)}, u32[]{:S(2)}) %collective-permute-start.13) | collective-permute-done | bytes 1048608 | tf_op jit(solution)/shard_map/ppermute | solution.py:28
  231.3 1.3 collective-permute-start.8
  233.3 5.1 %collective-permute-start.7 = (f32[2,4,64,512]{3,2,1,0:T(8,128)S(1)}, f32[2,4,64,512]{3,2,1,0:T(8,128)S(1)}, u32[]{:S(2)}, u32[]{:S(2)}) collective-permute-start(f32[2,4,64,512]{3,2,1,0:T(8,128)S(1)} %fusion.15), channel_id=1, source_target_pairs={{2,0},{4,2},{6,4},{8,6},{10,8},{12,10},{14,12},{16,14},{18,16},{20... | collective-permute-start | bytes 3145736 | tf_op jit(solution)/shard_map/ppermute | solution.py:28
  238.4 1.2 fusion.6
  240.8 35.3 %collective-permute-done.9 = f32[2,4,64,512]{3,2,1,0:T(8,128)S(1)} collective-permute-done((f32[2,4,64,512]{3,2,1,0:T(8,128)S(1)}, f32[2,4,64,512]{3,2,1,0:T(8,128)S(1)}, u32[]{:S(2)}, u32[]{:S(2)}) %collective-permute-start.9) | collective-permute-done | bytes 1048608 | tf_op jit(solution)/shard_map/ppermute | solution.py:28
  276.6 15.1 %collective-permute-done.7 = f32[2,4,64,512]{3,2,1,0:T(8,128)S(1)} collective-permute-done((f32[2,4,64,512]{3,2,1,0:T(8,128)S(1)}, f32[2,4,64,512]{3,2,1,0:T(8,128)S(1)}, u32[]{:S(2)}, u32[]{:S(2)}) %collective-permute-start.7) | collective-permute-done | bytes 1048608 | tf_op jit(solution)/shard_map/ppermute | solution.py:28
  291.7 2.2 fusion.23
  295.5 1.7 fusion
  297.6 3.3 convolution_convert_fusion
  301.0 81.7 %reduce-scatter.5.cloned.1.call-done = bf16[128,2048]{1,0:T(8,128)(2,1)} async-done(((bf16[256,2048]{1,0:T(8,128)(2,1)}), bf16[128,2048]{1,0:T(8,128)(2,1)}) %reduce-scatter.5.cloned.1.call-update) | async-done | bytes 524304 | tf_op jit(solution)/shard_map/reduce_scatter | solution.py:144
  382.7 1.4 fusion.8
  384.1 27.7 %reduce-scatter.3.cloned.1.call-done = bf16[128,2048]{1,0:T(8,128)(2,1)} async-done(((bf16[256,2048]{1,0:T(8,128)(2,1)}), bf16[128,2048]{1,0:T(8,128)(2,1)}) %reduce-scatter.3.cloned.1.call-update) | async-done | bytes 524304 | tf_op jit(solution)/shard_map/reduce_scatter | solution.py:96
  411.8 2.7 fusion.12
  (87 shorter events, 14.5 us)
Async XLA Ops:
  7.2 65.3 %copy-start = (bf16[2048,512]{1,0:T(8,128)(2,1)S(1)}, bf16[2048,512]{1,0:T(8,128)(2,1)}, u32[]{:S(2)}) copy-start(bf16[2048,512]{1,0:T(8,128)(2,1)} %param.15) | copy-start | bytes 6291460
  7.2 37.7 %all-gather.2.cloned.1.call-start = ((), (), s32[]{:S(2)}) async-start(), calls=%async_computation.3 | async-start | bytes 1572864 | tf_op jit(solution)/shard_map/all_gather | solution.py:41
  13.0 18.0 %all-to-all-start = ((bf16[2,128,2048]{2,1,0:T(8,128)(2,1)}), bf16[2,128,2048]{2,1,0:T(8,128)(2,1)S(1)}, u32[]{:S(2)}, u32[]{:S(2)}) async-start(bf16[2,128,2048]{2,1,0:T(8,128)(2,1)} %pad_maximum_fusion.1), calls=%async_computation.1 | async-start | bytes 2097152 | tf_op jit(solution)/shard_map/all_to_all | solution.py:14
  17.8 364.9 %reduce-scatter.5.cloned.1.call-start = ((), (), s32[]{:S(2)}) async-start(), calls=%async_computation.5 | async-start | bytes 1572864 | tf_op jit(solution)/shard_map/reduce_scatter | solution.py:144
  33.4 117.5 %copy-start.4 = (bf16[4,64,4,128]{3,2,1,0:T(4,128)(2,1)}, bf16[4,64,4,128]{3,2,1,0:T(4,128)(2,1)S(1)}, u32[]{:S(2)}) copy-start(bf16[4,64,4,128]{3,2,1,0:T(4,128)(2,1)S(1)} %reshape.222) | copy-start | bytes 786436
  44.9 2.8 copy-start.9
  44.9 2.8 copy-start.18
  47.7 22.8 %copy-start.7 = (bf16[256,512]{1,0:T(8,128)(2,1)}, bf16[256,512]{1,0:T(8,128)(2,1)S(1)}, u32[]{:S(2)}) copy-start(bf16[256,512]{1,0:T(8,128)(2,1)S(1)} %convolution_convert_fusion.4) | copy-start | bytes 786436
  48.4 26.0 %copy-start.8 = (bf16[256,512]{1,0:T(8,128)(2,1)}, bf16[256,512]{1,0:T(8,128)(2,1)S(1)}, u32[]{:S(2)}) copy-start(bf16[256,512]{1,0:T(8,128)(2,1)S(1)} %convolution_convert_fusion.5) | copy-start | bytes 786436
  49.3 25.9 %collective-permute-start = (bf16[2,256,512]{2,1,0:T(8,128)(2,1)}, bf16[2,256,512]{2,1,0:T(8,128)(2,1)}, u32[]{:S(2)}, u32[]{:S(2)}) collective-permute-start(bf16[2,256,512]{2,1,0:T(8,128)(2,1)} %pad_maximum_fusion.2), channel_id=1, source_target_pairs={{0,2},{2,4},{4,6},{6,8},{8,10},{10,12},{12,14},{14,16},{16,18},{18... | collective-permute-start | bytes 1572872 | tf_op jit(solution)/shard_map/ppermute | solution.py:28
  53.2 25.2 %collective-permute-start.1 = (bf16[2,256,512]{2,1,0:T(8,128)(2,1)}, bf16[2,256,512]{2,1,0:T(8,128)(2,1)S(1)}, u32[]{:S(2)}, u32[]{:S(2)}) collective-permute-start(bf16[2,256,512]{2,1,0:T(8,128)(2,1)} %pad_maximum_fusion.2), channel_id=1, source_target_pairs={{0,4},{2,6},{4,8},{6,10},{8,12},{10,14},{12,16},{14,18},{16,20},{1... | collective-permute-start | bytes 1572872 | tf_op jit(solution)/shard_map/ppermute | solution.py:28
  57.6 43.2 %collective-permute-start.2 = (bf16[2,256,512]{2,1,0:T(8,128)(2,1)}, bf16[2,256,512]{2,1,0:T(8,128)(2,1)}, u32[]{:S(2)}, u32[]{:S(2)}) collective-permute-start(bf16[2,256,512]{2,1,0:T(8,128)(2,1)} %pad_maximum_fusion.2), channel_id=1, source_target_pairs={{0,8},{2,10},{4,12},{6,14},{8,16},{10,18},{12,20},{14,22},{16,24},... | collective-permute-start | bytes 1572872 | tf_op jit(solution)/shard_map/ppermute | solution.py:28
  64.5 38.8 %collective-permute-start.3 = (bf16[2,256,512]{2,1,0:T(8,128)(2,1)}, bf16[2,256,512]{2,1,0:T(8,128)(2,1)}, u32[]{:S(2)}, u32[]{:S(2)}) collective-permute-start(bf16[2,256,512]{2,1,0:T(8,128)(2,1)} %pad_maximum_fusion.2), channel_id=1, source_target_pairs={{0,16},{2,18},{4,20},{6,22},{8,24},{10,26},{12,28},{14,30},{16,32}... | collective-permute-start | bytes 1572872 | tf_op jit(solution)/shard_map/ppermute | solution.py:28
  67.7 39.7 %collective-permute-start.4 = (bf16[2,256,512]{2,1,0:T(8,128)(2,1)}, bf16[2,256,512]{2,1,0:T(8,128)(2,1)}, u32[]{:S(2)}, u32[]{:S(2)}) collective-permute-start(bf16[2,256,512]{2,1,0:T(8,128)(2,1)} %pad_maximum_fusion.2), channel_id=1, source_target_pairs={{0,32},{2,34},{4,36},{6,38},{8,40},{10,42},{12,44},{14,46},{16,48}... | collective-permute-start | bytes 1572872 | tf_op jit(solution)/shard_map/ppermute | solution.py:28
  75.2 44.4 %collective-permute-start.5 = (bf16[2,256,512]{2,1,0:T(8,128)(2,1)}, bf16[2,256,512]{2,1,0:T(8,128)(2,1)}, u32[]{:S(2)}, u32[]{:S(2)}) collective-permute-start(bf16[2,256,512]{2,1,0:T(8,128)(2,1)} %pad_maximum_fusion.2), channel_id=1, source_target_pairs={{0,64},{2,66},{4,68},{6,70},{8,72},{10,74},{12,76},{14,78},{16,80}... | collective-permute-start | bytes 1572872 | tf_op jit(solution)/shard_map/ppermute | solution.py:28
  78.4 0.8 copy-start.16
  79.2 51.6 %collective-permute-start.6 = (bf16[2,256,512]{2,1,0:T(8,128)(2,1)}, bf16[2,256,512]{2,1,0:T(8,128)(2,1)}, u32[]{:S(2)}, u32[]{:S(2)}) collective-permute-start(bf16[2,256,512]{2,1,0:T(8,128)(2,1)} %pad_maximum_fusion.2), channel_id=1, source_target_pairs={{0,128},{2,130},{4,132},{6,134},{8,136},{10,138},{12,140},{14,142}... | collective-permute-start | bytes 1572872 | tf_op jit(solution)/shard_map/ppermute | solution.py:28
  145.6 3.1 copy-start.6
  145.6 3.1 copy-start.15
  148.6 1.5 copy-start.1
  150.9 3.3 copy-start.11
  154.2 2.0 copy-start.5
  205.8 25.5 %collective-permute-start.13 = (f32[2,4,64,512]{3,2,1,0:T(8,128)S(1)}, f32[2,4,64,512]{3,2,1,0:T(8,128)S(1)}, u32[]{:S(2)}, u32[]{:S(2)}) collective-permute-start(f32[2,4,64,512]{3,2,1,0:T(8,128)S(1)} %get-tuple-element.43), channel_id=1, source_target_pairs={{128,0},{130,2},{132,4},{134,6},{136,8},{138,10},{140,12},{142,14}... | collective-permute-start | bytes 3145736 | tf_op jit(solution)/shard_map/ppermute | solution.py:28
  207.1 26.1 %collective-permute-start.12 = (f32[2,4,64,512]{3,2,1,0:T(8,128)S(1)}, f32[2,4,64,512]{3,2,1,0:T(8,128)S(1)}, u32[]{:S(2)}, u32[]{:S(2)}) collective-permute-start(f32[2,4,64,512]{3,2,1,0:T(8,128)S(1)} %get-tuple-element.44), channel_id=1, source_target_pairs={{64,0},{66,2},{68,4},{70,6},{72,8},{74,10},{76,12},{78,14},{80,16}... | collective-permute-start | bytes 3145736 | tf_op jit(solution)/shard_map/ppermute | solution.py:28
  208.4 32.1 %collective-permute-start.11 = (f32[2,4,64,512]{3,2,1,0:T(8,128)S(1)}, f32[2,4,64,512]{3,2,1,0:T(8,128)S(1)}, u32[]{:S(2)}, u32[]{:S(2)}) collective-permute-start(f32[2,4,64,512]{3,2,1,0:T(8,128)S(1)} %get-tuple-element.39), channel_id=1, source_target_pairs={{32,0},{34,2},{36,4},{38,6},{40,8},{42,10},{44,12},{46,14},{48,16}... | collective-permute-start | bytes 3145736 | tf_op jit(solution)/shard_map/ppermute | solution.py:28
  209.7 31.0 %collective-permute-start.10 = (f32[2,4,64,512]{3,2,1,0:T(8,128)S(1)}, f32[2,4,64,512]{3,2,1,0:T(8,128)S(1)}, u32[]{:S(2)}, u32[]{:S(2)}) collective-permute-start(f32[2,4,64,512]{3,2,1,0:T(8,128)S(1)} %get-tuple-element.40), channel_id=1, source_target_pairs={{16,0},{18,2},{20,4},{22,6},{24,8},{26,10},{28,12},{30,14},{32,16}... | collective-permute-start | bytes 3145736 | tf_op jit(solution)/shard_map/ppermute | solution.py:28
  211.0 65.0 %collective-permute-start.9 = (f32[2,4,64,512]{3,2,1,0:T(8,128)S(1)}, f32[2,4,64,512]{3,2,1,0:T(8,128)S(1)}, u32[]{:S(2)}, u32[]{:S(2)}) collective-permute-start(f32[2,4,64,512]{3,2,1,0:T(8,128)S(1)} %get-tuple-element.41), channel_id=1, source_target_pairs={{8,0},{10,2},{12,4},{14,6},{16,8},{18,10},{20,12},{22,14},{24,16},... | collective-permute-start | bytes 3145736 | tf_op jit(solution)/shard_map/ppermute | solution.py:28
  212.6 25.8 %copy-start.2 = (bf16[1,4,640,512]{2,3,1,0:T(8,128)(2,1)S(1)}, bf16[1,4,640,512]{2,3,1,0:T(8,128)(2,1)}, u32[]{:S(2)}) copy-start(bf16[1,4,640,512]{2,3,1,0:T(8,128)(2,1)} %copy-done.1) | copy-start | bytes 7864324
  231.3 45.3 %collective-permute-start.8 = (f32[2,4,64,512]{3,2,1,0:T(8,128)S(1)}, f32[2,4,64,512]{3,2,1,0:T(8,128)S(1)}, u32[]{:S(2)}, u32[]{:S(2)}) collective-permute-start(f32[2,4,64,512]{3,2,1,0:T(8,128)S(1)} %get-tuple-element.42), channel_id=1, source_target_pairs={{4,0},{6,2},{8,4},{10,6},{12,8},{14,10},{16,12},{18,14},{20,16},{2... | collective-permute-start | bytes 3145736 | tf_op jit(solution)/shard_map/ppermute | solution.py:28
  233.3 58.4 %collective-permute-start.7 = (f32[2,4,64,512]{3,2,1,0:T(8,128)S(1)}, f32[2,4,64,512]{3,2,1,0:T(8,128)S(1)}, u32[]{:S(2)}, u32[]{:S(2)}) collective-permute-start(f32[2,4,64,512]{3,2,1,0:T(8,128)S(1)} %fusion.15), channel_id=1, source_target_pairs={{2,0},{4,2},{6,4},{8,6},{10,8},{12,10},{14,12},{16,14},{18,16},{20... | collective-permute-start | bytes 3145736 | tf_op jit(solution)/shard_map/ppermute | solution.py:28
  240.5 53.4 %copy-start.10 = (bf16[2048,512]{1,0:T(8,128)(2,1)S(1)}, bf16[2048,512]{1,0:T(8,128)(2,1)}, u32[]{:S(2)}) copy-start(bf16[2048,512]{1,0:T(8,128)(2,1)} %param.16) | copy-start | bytes 6291460
  293.9 1.6 copy-start.12
  295.5 1.8 copy-start.14
  297.3 85.4 %copy-start.3 = (bf16[128,2048]{1,0:T(8,128)(2,1)S(1)}, bf16[128,2048]{1,0:T(8,128)(2,1)}, u32[]{:S(2)}) copy-start(bf16[128,2048]{1,0:T(8,128)(2,1)} %param.13) | copy-start | bytes 1572868
  297.3 85.4 %copy-start.17 = (f32[2048]{0:T(1024)S(1)}, f32[2048]{0:T(1024)}, u32[]{:S(2)}) copy-start(f32[2048]{0:T(1024)} %param.14) | copy-start | bytes 24580
  297.3 114.4 %reduce-scatter.3.cloned.1.call-start = ((), (), s32[]{:S(2)}) async-start(), calls=%async_computation.4 | async-start | bytes 1572864 | tf_op jit(solution)/shard_map/reduce_scatter | solution.py:96
  297.6 114.2 %copy-start.13 = (bf16[128,2048]{1,0:T(8,128)(2,1)S(1)}, bf16[128,2048]{1,0:T(8,128)(2,1)}, u32[]{:S(2)}) copy-start(bf16[128,2048]{1,0:T(8,128)(2,1)} %param.19) | copy-start | bytes 1572868
Sparse Core Ops, SparseCore 0:
  10.8 34.0 all-gather.1
  297.4 85.2 reduce-scatter.4
  385.4 26.3 reduce-scatter.2
